TPU v7x, 256 devices: a whole 4x4x8 slice. The times are simulated.
256 devices in a mesh: prow: 8 (over z), pcol: 32 (over x, y, core).
Axes of the slice: x: 4, y: 4, z: 8, core: 2. Of those that a mesh axis runs over, the one named last changes fastest.
Arguments:
- matrix: bfloat16 [8, 2048, 2, 8192], P(None, 'prow', None, 'pcol'), may hold values from -6 to 6
- pivots: int32 [4, 256], replicated, may hold values from 0 to 16383, as said below
- lower_inverse: bfloat16 [4, 256, 256], replicated, as said below
- upper_inverse: bfloat16 [4, 256, 256], replicated, as said below
Outputs:
- factored: bfloat16 [8, 2048, 2, 8192], P(None, 'prow', None, 'pcol')
Inputs may be any that keep to these rules, and one draw needn't show every extreme that they name: For step s and each i, pivots[s, i] is either s * 256 + i or a row index of s * 256 + 256 or more; the pivots of one step that differ from s * 256 + i are distinct. lower_inverse[s] is unit lower triangular. upper_inverse[s] is upper triangular.
All inputs are finite; a program needn't handle non-finite values.
Results may differ from a plain program's by a relative error of at most 0.0071.
Values may be sent and summed in bfloat16 or wider, within the bound.
A program may use at most 64 MiB of HBM per device.

v0:
```python
import jax
import jax.numpy as jnp
from jax import lax
from jax.sharding import PartitionSpec as P


def spread(value, axis, source):
    kept = jnp.where(lax.axis_index(axis) == source, value, 0).astype(value.dtype)
    return lax.psum(kept, axis)


def local(matrix, pivots, lower_inverse, upper_inverse):
    row_blocks = matrix.shape[0]
    block_size = matrix.shape[1]
    col_blocks = matrix.shape[2]
    local_rows = row_blocks * block_size
    local_cols = col_blocks * block_size
    matrix_loc = matrix.reshape(local_rows, local_cols)
    row_count = lax.axis_size("prow")
    col_count = lax.axis_size("pcol")
    my_row = lax.axis_index("prow")
    my_col = lax.axis_index("pcol")
    row_iota = jnp.arange(local_rows, dtype=jnp.int32)
    col_iota = jnp.arange(local_cols, dtype=jnp.int32)
    global_row = (row_iota // block_size * row_count + my_row) * block_size + row_iota % block_size
    global_col = (col_iota // block_size * col_count + my_col) * block_size + col_iota % block_size
    for step_num in range(pivots.shape[0]):
        begin_at = step_num * block_size
        trail_at = begin_at + block_size
        diag_root = step_num % row_count
        diag_local = step_num // row_count * block_size
        panel_root = step_num % col_count
        panel_local = step_num // col_count * block_size
        targets = begin_at + jnp.arange(block_size, dtype=jnp.int32)
        chosen = pivots[step_num]
        chosen_block = chosen // block_size
        chosen_owner = chosen_block % row_count
        is_mine = chosen_owner == my_row
        chosen_local = chosen_block // row_count * block_size + chosen % block_size
        picked = jnp.take(matrix_loc, jnp.where(is_mine, chosen_local, 0), axis=0)
        picked = jnp.where(is_mine[:, None], picked, jnp.zeros_like(picked))
        diag_rows = matrix_loc[diag_local : diag_local + block_size]
        gathered = lax.all_gather(picked, "prow", axis=0, tiled=True)
        stacked = gathered.reshape(row_count, block_size, local_cols)
        owner_hit = jnp.arange(row_count, dtype=jnp.int32)[:, None] == chosen_owner[None, :]
        new_rows = jnp.sum(
            jnp.where(owner_hit[:, :, None], stacked, jnp.zeros_like(stacked)), axis=0
        )
        old_diag = spread(diag_rows, "prow", diag_root)
        moved_rows = is_mine & (chosen != targets)
        matrix_loc = matrix_loc.at[jnp.where(moved_rows, chosen_local, local_rows)].set(
            old_diag, mode="drop"
        )
        diag_after = matrix_loc[diag_local : diag_local + block_size]
        matrix_loc = matrix_loc.at[diag_local : diag_local + block_size].set(
            jnp.where(my_row == diag_root, new_rows, diag_after)
        )
        upper_full = jnp.dot(
            lower_inverse[step_num], new_rows, preferred_element_type=jnp.float32
        ).astype(jnp.bfloat16)
        col_live = global_col >= trail_at
        upper_use = jnp.where(col_live[None, :], upper_full, jnp.zeros_like(upper_full))
        panel_own = matrix_loc[:, panel_local : panel_local + block_size]
        received = spread(panel_own, "pcol", panel_root)
        left_full = jnp.dot(
            received, upper_inverse[step_num], preferred_element_type=jnp.float32
        ).astype(jnp.bfloat16)
        row_live = global_row >= trail_at
        left_use = jnp.where(row_live[:, None], left_full, jnp.zeros_like(left_full))
        matrix_loc = (
            matrix_loc.astype(jnp.float32)
            - jnp.dot(left_use, upper_use, preferred_element_type=jnp.float32)
        ).astype(jnp.bfloat16)
        panel_now = matrix_loc[:, panel_local : panel_local + block_size]
        panel_put = jnp.where(row_live[:, None] & (my_col == panel_root), left_full, panel_now)
        matrix_loc = matrix_loc.at[:, panel_local : panel_local + block_size].set(panel_put)
        diag_now = matrix_loc[diag_local : diag_local + block_size]
        diag_put = jnp.where(col_live[None, :] & (my_row == diag_root), upper_full, diag_now)
        matrix_loc = matrix_loc.at[diag_local : diag_local + block_size].set(diag_put)
    return matrix_loc.reshape(matrix.shape)


def solution(mesh):
    placed = (P(None, "prow", None, "pcol"), P(), P(), P())
    return jax.shard_map(
        local, mesh=mesh, in_specs=placed, out_specs=P(None, "prow", None, "pcol"), check_vma=False
    )
```

profile of v0, /device:TPU:1, one launch (start us, length us, event | category | flops | bytes accessed | tf_op | source)
XLA Modules:
  0.0 982.3 jit_solution(12199594610326055330)
XLA Ops:
  14.4 66.9 %all-reduce.9.cloned.1.call-done = bf16[256,512]{1,0:T(8,128)(2,1)} async-done(((bf16[256,512]{1,0:T(8,128)(2,1)}), bf16[256,512]{1,0:T(8,128)(2,1)}) %all-reduce.9.cloned.1.call-update) | async-done | bytes 262160 | tf_op jit(solution)/shard_map/psum | solution.py:9
  81.3 3.1 scatter_fusion
  84.4 38.9 %all-gather.5.cloned.1.call-done = bf16[2048,512]{1,0:T(8,128)(2,1)} async-done(((bf16[256,512]{1,0:T(8,128)(2,1)}), bf16[2048,512]{1,0:T(8,128)(2,1)}) %all-gather.5.cloned.1.call-update) | async-done | bytes 2097168 | tf_op jit(solution)/shard_map/all_gather | solution.py:43
  126.7 118.0 %all-reduce.11.cloned.1.call-done = bf16[2048,256]{1,0:T(8,128)(2,1)} async-done(((bf16[2048,256]{1,0:T(8,128)(2,1)}), bf16[2048,256]{1,0:T(8,128)(2,1)}) %all-reduce.11.cloned.1.call-update) | async-done | bytes 1048592 | tf_op jit(solution)/shard_map/psum | solution.py:9
  248.4 3.4 fusion.4
  253.7 3.1 gather_fusion.1
  257.8 63.7 %all-reduce.13.cloned.1.call-done = bf16[256,512]{1,0:T(8,128)(2,1)} async-done(((bf16[256,512]{1,0:T(8,128)(2,1)}), bf16[256,512]{1,0:T(8,128)(2,1)}) %all-reduce.13.cloned.1.call-update) | async-done | bytes 262160 | tf_op jit(solution)/shard_map/psum | solution.py:9
  321.5 5.2 scatter_fusion.1
  326.7 36.7 %all-gather.7.cloned.1.call-done = bf16[2048,512]{1,0:T(8,128)(2,1)} async-done(((bf16[256,512]{1,0:T(8,128)(2,1)}), bf16[2048,512]{1,0:T(8,128)(2,1)}) %all-gather.7.cloned.1.call-update) | async-done | bytes 2097168 | tf_op jit(solution)/shard_map/all_gather | solution.py:43
  367.0 2.3 slice_select_fusion.2
  369.6 118.0 %all-reduce.15.cloned.1.call-done = bf16[2048,256]{1,0:T(8,128)(2,1)} async-done(((bf16[2048,256]{1,0:T(8,128)(2,1)}), bf16[2048,256]{1,0:T(8,128)(2,1)}) %all-reduce.15.cloned.1.call-update) | async-done | bytes 1048592 | tf_op jit(solution)/shard_map/psum | solution.py:9
  489.3 2.3 subtract_convert_fusion.2
  496.2 65.4 %all-reduce.17.cloned.1.call-done = bf16[256,512]{1,0:T(8,128)(2,1)} async-done(((bf16[256,512]{1,0:T(8,128)(2,1)}), bf16[256,512]{1,0:T(8,128)(2,1)}) %all-reduce.17.cloned.1.call-update) | async-done | bytes 262160 | tf_op jit(solution)/shard_map/psum | solution.py:9
  561.6 3.1 scatter_fusion.2
  564.7 38.9 %all-gather.9.cloned.1.call-done = bf16[2048,512]{1,0:T(8,128)(2,1)} async-done(((bf16[256,512]{1,0:T(8,128)(2,1)}), bf16[2048,512]{1,0:T(8,128)(2,1)}) %all-gather.9.cloned.1.call-update) | async-done | bytes 2097168 | tf_op jit(solution)/shard_map/all_gather | solution.py:43
  607.0 118.0 %all-reduce.19.cloned.1.call-done = bf16[2048,256]{1,0:T(8,128)(2,1)} async-done(((bf16[2048,256]{1,0:T(8,128)(2,1)}), bf16[2048,256]{1,0:T(8,128)(2,1)}) %all-reduce.19.cloned.1.call-update) | async-done | bytes 1048592 | tf_op jit(solution)/shard_map/psum | solution.py:9
  728.6 3.4 fusion.6
  734.0 3.1 gather_fusion.3
  738.0 63.7 %all-reduce.21.cloned.1.call-done = bf16[256,512]{1,0:T(8,128)(2,1)} async-done(((bf16[256,512]{1,0:T(8,128)(2,1)}), bf16[256,512]{1,0:T(8,128)(2,1)}) %all-reduce.21.cloned.1.call-update) | async-done | bytes 262160 | tf_op jit(solution)/shard_map/psum | solution.py:9
  801.7 5.2 scatter_fusion.3
  806.9 36.8 %all-gather.11.cloned.1.call-done = bf16[2048,512]{1,0:T(8,128)(2,1)} async-done(((bf16[256,512]{1,0:T(8,128)(2,1)}), bf16[2048,512]{1,0:T(8,128)(2,1)}) %all-gather.11.cloned.1.call-update) | async-done | bytes 2097168 | tf_op jit(solution)/shard_map/all_gather | solution.py:43
  847.4 2.3 slice_select_fusion
  850.0 118.0 %all-reduce.23.cloned.1.call-done = bf16[2048,256]{1,0:T(8,128)(2,1)} async-done(((bf16[2048,256]{1,0:T(8,128)(2,1)}), bf16[2048,256]{1,0:T(8,128)(2,1)}) %all-reduce.23.cloned.1.call-update) | async-done | bytes 1048592 | tf_op jit(solution)/shard_map/psum | solution.py:9
  969.7 2.3 subtract_convert_fusion
  (93 shorter events, 46.6 us)
Async XLA Ops:
  6.5 74.8 %all-reduce.9.cloned.1.call-start = ((), (), s32[]{:S(2)}) async-start(), calls=%async_computation | async-start | bytes 524288 | tf_op jit(solution)/shard_map/psum | solution.py:9
  8.5 114.9 %all-gather.5.cloned.1.call-start = ((), (), s32[]{:S(2)}) async-start(), calls=%async_computation.1 | async-start | bytes 2359296 | tf_op jit(solution)/shard_map/all_gather | solution.py:43
  11.5 2.8 copy-start.1
  13.5 231.2 %all-reduce.11.cloned.1.call-start = ((), (), s32[]{:S(2)}) async-start(), calls=%async_computation.2 | async-start | bytes 2097152 | tf_op jit(solution)/shard_map/psum | solution.py:9
  125.2 1.3 copy-start
  126.4 195.1 %all-reduce.13.cloned.1.call-start = ((), (), s32[]{:S(2)}) async-start(), calls=%async_computation.3 | async-start | bytes 524288 | tf_op jit(solution)/shard_map/psum | solution.py:9
  253.6 109.7 %all-gather.7.cloned.1.call-start = ((), (), s32[]{:S(2)}) async-start(), calls=%async_computation.4 | async-start | bytes 2359296 | tf_op jit(solution)/shard_map/all_gather | solution.py:43
  257.6 230.0 %all-reduce.15.cloned.1.call-start = ((), (), s32[]{:S(2)}) async-start(), calls=%async_computation.5 | async-start | bytes 2097152 | tf_op jit(solution)/shard_map/psum | solution.py:9
  369.3 192.3 %all-reduce.17.cloned.1.call-start = ((), (), s32[]{:S(2)}) async-start(), calls=%async_computation.6 | async-start | bytes 524288 | tf_op jit(solution)/shard_map/psum | solution.py:9
  493.8 109.8 %all-gather.9.cloned.1.call-start = ((), (), s32[]{:S(2)}) async-start(), calls=%async_computation.7 | async-start | bytes 2359296 | tf_op jit(solution)/shard_map/all_gather | solution.py:43
  496.1 228.9 %all-reduce.19.cloned.1.call-start = ((), (), s32[]{:S(2)}) async-start(), calls=%async_computation.8 | async-start | bytes 2097152 | tf_op jit(solution)/shard_map/psum | solution.py:9
  606.7 195.1 %all-reduce.21.cloned.1.call-start = ((), (), s32[]{:S(2)}) async-start(), calls=%async_computation.9 | async-start | bytes 524288 | tf_op jit(solution)/shard_map/psum | solution.py:9
  733.9 109.9 %all-gather.11.cloned.1.call-start = ((), (), s32[]{:S(2)}) async-start(), calls=%async_computation.10 | async-start | bytes 2359296 | tf_op jit(solution)/shard_map/all_gather | solution.py:43
  737.9 230.1 %all-reduce.23.cloned.1.call-start = ((), (), s32[]{:S(2)}) async-start(), calls=%async_computation.11 | async-start | bytes 2097152 | tf_op jit(solution)/shard_map/psum | solution.py:9
Sparse Core Ops, SparseCore 0:
  9.6 71.6 all-reduce.8
  83.1 40.1 all-gather.4
  126.6 118.0 all-reduce.10
  253.8 67.6 all-reduce.12
  323.1 40.1 all-gather.6
  369.4 118.1 all-reduce.14
  494.0 67.5 all-reduce.16
  563.4 40.1 all-gather.8
  606.9 118.0 all-reduce.18
  734.0 67.6 all-reduce.20
  803.5 40.1 all-gather.10
  849.8 118.1 all-reduce.22
where the time goes:
time: 983 us; the launch traced here: 982 us
  waiting for transfers between devices  883 us (90%)
  other arithmetic  38.6 us (4%)
  local copies, waits for them, and re-layouts  29.8 us (3%)
  matrix products  16 us (2%)
  between operations  13.9 us (1%)
    psum x8, waiting for transfers between devices, spread(): return lax.psum(kept, axis)  732 us
    all_gather x4, waiting for transfers between devices, local(): gathered = lax.all_gather(picked, 'prow', axis=0, tiled=True)  151 us
  transfers between devices with their start and end apart: 12, of which 12 were waited for; matrix products, arithmetic and copies ran while one was open for 3% of the time, Pallas kernels for 0%

commit v1 on v0

--- a/solution.py
+++ b/solution.py
@@ -6,7 +6,11 @@
 
 def spread(value, axis, source):
     kept = jnp.where(lax.axis_index(axis) == source, value, 0).astype(value.dtype)
-    return lax.psum(kept, axis)
+
+    def proceed_the_entries(field, named_axis):
+        return jnp.sum(lax.all_gather(field, named_axis), axis=0)
+
+    return proceed_the_entries(kept, axis)
 
 
 def local(matrix, pivots, lower_inverse, upper_inverse):

time: 983 us -> 917 us (0.933)
  waiting for transfers between devices: 883 us -> 764 us
  other arithmetic: 38.6 us -> 91.8 us
    psum x8 -> x0, waiting for transfers between devices: 732 us -> none  [spread(): return lax.psum(kept, axis)]
    all_gather x0 -> x8, waiting for transfers between devices: none -> 620 us  [proceed_the_entries(): return jnp.sum(lax.all_gather(field, named_axis), axis=0)]
    reduce_sum x0 -> x8, other arithmetic: none -> 53.5 us  [proceed_the_entries(): return jnp.sum(lax.all_gather(field, named_axis), axis=0)]
  transfers between devices with their start and end apart: 12 -> 12, of which waited for: 12 -> 12; matrix products, arithmetic and copies ran while one was open for 3% -> 4% of each run, Pallas kernels for 0% -> 0%
where the time goes in v1:
time: 917 us; the launch traced here: 916 us
  waiting for transfers between devices  764 us (83%)
  other arithmetic  91.8 us (10%)
  local copies, waits for them, and re-layouts  28.4 us (3%)
  matrix products  16.5 us (2%)
  between operations  14 us (2%)
    all_gather x8, waiting for transfers between devices, proceed_the_entries(): return jnp.sum(lax.all_gather(field, named_axis), axis=0)  620 us
    all_gather x4, waiting for transfers between devices, local(): gathered = lax.all_gather(picked, 'prow', axis=0, tiled=True)  144 us
    reduce_sum x8, other arithmetic, proceed_the_entries(): return jnp.sum(lax.all_gather(field, named_axis), axis=0)  53.5 us
  transfers between devices with their start and end apart: 12, of which 12 were waited for; matrix products, arithmetic and copies ran while one was open for 4% of the time, Pallas kernels for 0%

profile of v1, /device:TPU:1, one launch (start us, length us, event | category | flops | bytes accessed | tf_op | source)
XLA Modules:
  0.0 915.7 jit_solution(3823962373879532306)
XLA Ops:
  13.8 38.3 %all-gather.22.cloned.1.call-done = bf16[2048,512]{1,0:T(8,128)(2,1)} async-done(((bf16[256,512]{1,0:T(8,128)(2,1)}), bf16[2048,512]{1,0:T(8,128)(2,1)}) %all-gather.22.cloned.1.call-update) | async-done | bytes 2097168 | tf_op jit(solution)/shard_map/all_gather | solution.py:47
  54.0 39.4 %all-gather.20.cloned.1.call-done = bf16[8,256,512]{2,1,0:T(8,128)(2,1)} async-done(((bf16[1,256,512]{2,1,0:T(8,128)(2,1)}), bf16[8,256,512]{2,1,0:T(8,128)(2,1)}) %all-gather.20.cloned.1.call-update) | async-done | bytes 2097168 | tf_op jit(solution)/shard_map/all_gather | solution.py:11
  95.3 2.7 scatter_fusion
  101.1 120.1 %all-gather.30.cloned.1.call-done = bf16[65536,256]{1,0:T(8,128)(2,1)} async-done(((bf16[2048,256]{1,0:T(8,128)(2,1)}), bf16[65536,256]{1,0:T(8,128)(2,1)}) %all-gather.30.cloned.1.call-update) | async-done | bytes 33554448 | tf_op jit(solution)/shard_map/all_gather | solution.py:11
  221.2 11.4 %reduce_sum.146 = bf16[2048,256]{1,0:T(8,128)(2,1)S(1)} reduce(bf16[32,2048,256]{2,1,0:T(8,128)(2,1)} %bitcast.130, bf16[]{:T(256)} %constant.520.clone.1), dimensions={0}, to_apply=%region_3.5 | reduce | flops 16252928 | bytes 34603008 | tf_op jit(solution)/shard_map/reduce_sum | solution.py:11
  236.0 3.4 fusion.4
  241.3 3.1 gather_fusion.1
  245.3 31.7 %all-gather.32.cloned.1.call-done = bf16[2048,512]{1,0:T(8,128)(2,1)} async-done(((bf16[256,512]{1,0:T(8,128)(2,1)}), bf16[2048,512]{1,0:T(8,128)(2,1)}) %all-gather.32.cloned.1.call-update) | async-done | bytes 2097168 | tf_op jit(solution)/shard_map/all_gather | solution.py:11
  278.9 4.8 scatter_fusion.1
  283.7 34.3 %all-gather.24.cloned.1.call-done = bf16[2048,512]{1,0:T(8,128)(2,1)} async-done(((bf16[256,512]{1,0:T(8,128)(2,1)}), bf16[2048,512]{1,0:T(8,128)(2,1)}) %all-gather.24.cloned.1.call-update) | async-done | bytes 2097168 | tf_op jit(solution)/shard_map/all_gather | solution.py:47
  324.6 121.5 %all-gather.34.cloned.1.call-done = bf16[65536,256]{1,0:T(8,128)(2,1)} async-done(((bf16[2048,256]{1,0:T(8,128)(2,1)}), bf16[65536,256]{1,0:T(8,128)(2,1)}) %all-gather.34.cloned.1.call-update) | async-done | bytes 33554448 | tf_op jit(solution)/shard_map/all_gather | solution.py:11
  446.0 11.4 %reduce_sum.149 = bf16[2048,256]{1,0:T(8,128)(2,1)S(1)} reduce(bf16[32,2048,256]{2,1,0:T(8,128)(2,1)} %bitcast.131, bf16[]{:T(256)} %constant.520.clone.1), dimensions={0}, to_apply=%region_8.10 | reduce | flops 16252928 | bytes 34603008 | tf_op jit(solution)/shard_map/reduce_sum | solution.py:11
  465.5 33.6 %all-gather.36.cloned.1.call-done = bf16[2048,512]{1,0:T(8,128)(2,1)} async-done(((bf16[256,512]{1,0:T(8,128)(2,1)}), bf16[2048,512]{1,0:T(8,128)(2,1)}) %all-gather.36.cloned.1.call-update) | async-done | bytes 2097168 | tf_op jit(solution)/shard_map/all_gather | solution.py:11
  501.1 2.7 scatter_fusion.2
  503.8 36.6 %all-gather.26.cloned.1.call-done = bf16[2048,512]{1,0:T(8,128)(2,1)} async-done(((bf16[256,512]{1,0:T(8,128)(2,1)}), bf16[2048,512]{1,0:T(8,128)(2,1)}) %all-gather.26.cloned.1.call-update) | async-done | bytes 2097168 | tf_op jit(solution)/shard_map/all_gather | solution.py:47
  543.8 121.7 %all-gather.38.cloned.1.call-done = bf16[65536,256]{1,0:T(8,128)(2,1)} async-done(((bf16[2048,256]{1,0:T(8,128)(2,1)}), bf16[65536,256]{1,0:T(8,128)(2,1)}) %all-gather.38.cloned.1.call-update) | async-done | bytes 33554448 | tf_op jit(solution)/shard_map/all_gather | solution.py:11
  665.4 11.4 %reduce_sum.152 = bf16[2048,256]{1,0:T(8,128)(2,1)S(1)} reduce(bf16[32,2048,256]{2,1,0:T(8,128)(2,1)} %bitcast.132, bf16[]{:T(256)} %constant.520.clone.1), dimensions={0}, to_apply=%region_12.14 | reduce | flops 16252928 | bytes 34603008 | tf_op jit(solution)/shard_map/reduce_sum | solution.py:11
  680.2 3.4 fusion.6
  685.5 3.1 gather_fusion.3
  689.5 31.7 %all-gather.40.cloned.1.call-done = bf16[2048,512]{1,0:T(8,128)(2,1)} async-done(((bf16[256,512]{1,0:T(8,128)(2,1)}), bf16[2048,512]{1,0:T(8,128)(2,1)}) %all-gather.40.cloned.1.call-update) | async-done | bytes 2097168 | tf_op jit(solution)/shard_map/all_gather | solution.py:11
  723.1 4.8 scatter_fusion.3
  727.9 34.5 %all-gather.28.cloned.1.call-done = bf16[2048,512]{1,0:T(8,128)(2,1)} async-done(((bf16[256,512]{1,0:T(8,128)(2,1)}), bf16[2048,512]{1,0:T(8,128)(2,1)}) %all-gather.28.cloned.1.call-update) | async-done | bytes 2097168 | tf_op jit(solution)/shard_map/all_gather | solution.py:47
  769.5 120.8 %all-gather.42.cloned.1.call-done = bf16[65536,256]{1,0:T(8,128)(2,1)} async-done(((bf16[2048,256]{1,0:T(8,128)(2,1)}), bf16[65536,256]{1,0:T(8,128)(2,1)}) %all-gather.42.cloned.1.call-update) | async-done | bytes 33554448 | tf_op jit(solution)/shard_map/all_gather | solution.py:11
  890.3 11.4 %reduce_sum.155 = bf16[2048,256]{1,0:T(8,128)(2,1)S(1)} reduce(bf16[32,2048,256]{2,1,0:T(8,128)(2,1)} %bitcast.133, bf16[]{:T(256)} %constant.520.clone.1), dimensions={0}, to_apply=%region_16.18 | reduce | flops 16252928 | bytes 34603008 | tf_op jit(solution)/shard_map/reduce_sum | solution.py:11
  (101 shorter events, 64.0 us)
Async XLA Ops:
  6.5 45.6 %all-gather.22.cloned.1.call-start = ((), (), s32[]{:S(2)}) async-start(), calls=%async_computation.1 | async-start | bytes 2359296 | tf_op jit(solution)/shard_map/all_gather | solution.py:47
  9.5 4.2 copy-start.1
  11.5 81.8 %all-gather.20.cloned.1.call-start = ((), (), s32[]{:S(2)}) async-start(), calls=%async_computation | async-start | bytes 2359296 | tf_op jit(solution)/shard_map/all_gather | solution.py:11
  13.6 207.6 %all-gather.30.cloned.1.call-start = ((), (), s32[]{:S(2)}) async-start(), calls=%async_computation.5 | async-start | bytes 34603008 | tf_op jit(solution)/shard_map/all_gather | solution.py:11
  99.2 177.8 %all-gather.32.cloned.1.call-start = ((), (), s32[]{:S(2)}) async-start(), calls=%async_computation.6 | async-start | bytes 2359296 | tf_op jit(solution)/shard_map/all_gather | solution.py:11
  241.2 76.9 %all-gather.24.cloned.1.call-start = ((), (), s32[]{:S(2)}) async-start(), calls=%async_computation.2 | async-start | bytes 2359296 | tf_op jit(solution)/shard_map/all_gather | solution.py:47
  245.2 200.9 %all-gather.34.cloned.1.call-start = ((), (), s32[]{:S(2)}) async-start(), calls=%async_computation.7 | async-start | bytes 34603008 | tf_op jit(solution)/shard_map/all_gather | solution.py:11
  319.9 4.4 copy-start
  324.0 175.1 %all-gather.36.cloned.1.call-start = ((), (), s32[]{:S(2)}) async-start(), calls=%async_computation.8 | async-start | bytes 2359296 | tf_op jit(solution)/shard_map/all_gather | solution.py:11
  463.4 77.0 %all-gather.26.cloned.1.call-start = ((), (), s32[]{:S(2)}) async-start(), calls=%async_computation.3 | async-start | bytes 2359296 | tf_op jit(solution)/shard_map/all_gather | solution.py:47
  465.5 200.0 %all-gather.38.cloned.1.call-start = ((), (), s32[]{:S(2)}) async-start(), calls=%async_computation.9 | async-start | bytes 34603008 | tf_op jit(solution)/shard_map/all_gather | solution.py:11
  543.4 177.8 %all-gather.40.cloned.1.call-start = ((), (), s32[]{:S(2)}) async-start(), calls=%async_computation.10 | async-start | bytes 2359296 | tf_op jit(solution)/shard_map/all_gather | solution.py:11
  685.4 77.0 %all-gather.28.cloned.1.call-start = ((), (), s32[]{:S(2)}) async-start(), calls=%async_computation.4 | async-start | bytes 2359296 | tf_op jit(solution)/shard_map/all_gather | solution.py:47
  689.4 200.9 %all-gather.42.cloned.1.call-start = ((), (), s32[]{:S(2)}) async-start(), calls=%async_computation.11 | async-start | bytes 34603008 | tf_op jit(solution)/shard_map/all_gather | solution.py:11
Sparse Core Ops, SparseCore 0:
  11.7 40.4 all-gather.21
  53.9 39.4 all-gather.19
  99.3 121.8 all-gather.29
  241.3 35.6 all-gather.31
  278.6 39.4 all-gather.23
  324.2 121.8 all-gather.33
  463.5 35.6 all-gather.35
  500.9 39.4 all-gather.25
  543.5 121.8 all-gather.37
  685.5 35.6 all-gather.39
  723.0 39.4 all-gather.27
  768.4 121.8 all-gather.41
